TPU v7x, 512 devices: a whole 4x8x8 slice. The times are simulated.
512 devices in a mesh: vocab: 64 (over y, x, core), width: 8 (over z).
Axes of the slice: x: 4, y: 8, z: 8, core: 2. Of those that a mesh axis runs over, the one named last changes fastest.
Arguments:
- hidden: bfloat16 [8192, 2048], P('vocab', 'width'), may hold values from -400 to 400
- norm_gain: bfloat16 [2048], P('width'), may hold values from 0.5 to 1.5
- head_weight: bfloat16 [102400, 2048], P('vocab', 'width'), may hold values from -1 to 1
- targets: int32 [8192], P(('vocab', 'width')), may hold values from 0 to 102399
- pad_mask: int32 [8192], P(('vocab', 'width')), may hold values 0 or 1
- lengths: int32 [64], replicated, may hold values from 1 to 2048, 8192 in all
Outputs:
- entropy: float32 [8192], P(('vocab', 'width'))
- token_logprob: float32 [8192], P(('vocab', 'width'))
- seq_score: float32 [64], replicated
Inputs may be any that keep to these rules, and one draw needn't show every extreme that they name: The lengths sum to 8192.
All inputs are finite; a program needn't handle non-finite values. No bound on the sum of `pad_mask` on one device may be relied on, other than what follows from the above.
Results may differ from a plain program's by a relative error of at most 0.0031.
Values may be sent and summed in bfloat16 or wider, within the bound.
A program may use at most 64 MiB of HBM per device.

v0:
```python
import math
import jax
import jax.numpy as jnp
from jax import lax
from jax.sharding import PartitionSpec as P

epsilon = 1e-06


def merged_2(value, axis, join):
    pieces = jax.tree.map(lambda part: lax.all_gather(part, axis), value)
    head = jax.tree.map(lambda part: part[0], pieces)
    tail = jax.tree.map(lambda part: part[1:], pieces)
    total, _ = lax.scan(lambda total, piece: (join(total, piece), None), head, tail)
    return total


def summarize(logits, block_ids, first_col):
    peak = jnp.max(logits, axis=1)
    shifted = logits - peak[:, None]
    weights = jnp.exp(shifted)
    exp_total = jnp.sum(weights, axis=1)
    spread = jnp.sum(weights * shifted, axis=1)
    columns = first_col + lax.iota(jnp.int32, logits.shape[1])
    target_logit = jnp.sum(jnp.where(columns[None, :] == block_ids[:, None], logits, 0.0), axis=1)
    return (peak, exp_total, spread, target_logit)


def combine(earlier, later):
    peak = jnp.maximum(earlier[0], later[0])
    left_lift = jnp.exp(earlier[0] - peak)
    right_lift = jnp.exp(later[0] - peak)
    exp_total = earlier[1] * left_lift + later[1] * right_lift
    spread = left_lift * (earlier[2] + (earlier[0] - peak) * earlier[1]) + right_lift * (
        later[2] + (later[0] - peak) * later[1]
    )
    return (peak, exp_total, spread, earlier[3] + later[3])


def per_device(hidden, norm_gain, head_weight, targets, pad_mask, lengths):
    width_count = lax.axis_size("width")
    own_count = targets.shape[0]
    values = hidden.astype(jnp.float32)
    energy = lax.psum(jnp.sum(values * values, axis=1), "width")
    inv_rms = lax.rsqrt(energy / (hidden.shape[1] * width_count) + epsilon)
    normed = (values * inv_rms[:, None] * norm_gain.astype(jnp.float32)[None, :]).astype(
        jnp.bfloat16
    )
    full_rows = lax.all_to_all(normed, "width", split_axis=0, concat_axis=1, tiled=True)
    gathered, gathered_ids = (
        lax.all_gather(full_rows, "vocab", axis=0, tiled=True),
        lax.all_gather(targets, "vocab", axis=0, tiled=True),
    )
    col_count = head_weight.shape[0]
    first_col = lax.axis_index("vocab") * col_count
    total_rows = gathered.shape[0]
    block_rows = math.gcd(total_rows, 512)
    contract = (((1,), (1,)), ((), ()))
    head_full = lax.all_gather(head_weight, "width", axis=1, tiled=True)

    def per_block(inputs):
        logits = lax.dot_general(inputs[0], head_full, contract, preferred_element_type=jnp.float32)
        return summarize(logits, inputs[1], first_col)

    blocked = lax.map(
        per_block,
        (gathered.reshape(-1, block_rows, gathered.shape[1]), gathered_ids.reshape(-1, block_rows)),
    )
    statistics = (
        blocked[0].reshape(-1),
        blocked[1].reshape(-1),
        blocked[2].reshape(-1),
        blocked[3].reshape(-1),
    )
    merged = merged_2(statistics, "vocab", combine)
    own_start = lax.axis_index("vocab") * own_count
    peak = lax.dynamic_slice_in_dim(merged[0], own_start, own_count, 0)
    exp_total = lax.dynamic_slice_in_dim(merged[1], own_start, own_count, 0)
    spread = lax.dynamic_slice_in_dim(merged[2], own_start, own_count, 0)
    target_logit = lax.dynamic_slice_in_dim(merged[3], own_start, own_count, 0)
    kept_mask = pad_mask.astype(jnp.float32)
    log_total = jnp.log(exp_total)
    entropy = kept_mask * (log_total - spread / exp_total)
    token_logprob = kept_mask * (target_logit - peak - log_total)
    device_index = lax.axis_index("vocab") * width_count + lax.axis_index("width")
    token_index = device_index * own_count + lax.iota(jnp.int32, own_count)
    seq_ends = jnp.cumsum(lengths)
    seq_starts = seq_ends - lengths
    member = (
        (token_index[:, None] >= seq_starts[None, :]) & (token_index[:, None] < seq_ends[None, :])
    ).astype(jnp.float32)
    partial_value = jnp.sum(member * token_logprob[:, None], axis=0)
    seq_score = lax.psum(partial_value, ("vocab", "width")) / lengths.astype(jnp.float32)
    return (entropy, token_logprob, seq_score)


def solution(mesh):
    placed = (
        P("vocab", "width"),
        P("width"),
        P("vocab", "width"),
        P(("vocab", "width")),
        P(("vocab", "width")),
        P(),
    )
    return jax.shard_map(
        per_device,
        mesh=mesh,
        in_specs=placed,
        out_specs=(P(("vocab", "width")), P(("vocab", "width")), P()),
        check_vma=False,
    )
```

profile of v0, /device:TPU:1, one launch (start us, length us, event | category | flops | bytes accessed | tf_op | source)
XLA Modules:
  0.0 491.1 jit_solution(4575408305845917003)
XLA Ops:
  7.2 0.0 all-gather.7.cloned.1.call-start
  7.2 0.9 fusion.5
  8.2 20.3 %psum.14 = f32[128]{0:T(128)S(1)} all-reduce(f32[128]{0:T(128)S(1)} %fusion.5), channel_id=1, replica_groups=mesh['vocab'=64,'width'=8] {'width'}, use_global_device_ids=true, to_apply=%region_1.0 | all-reduce | flops 128 | bytes 1024 | tf_op jit(solution)/shard_map/psum | solution.py:44
  28.4 0.7 convert_element_type.18
  29.1 0.9 fusion.7
  30.0 9.6 %all_to_all.19 = bf16[8,16,256]{2,1,0:T(8,128)(2,1)S(1)} all-to-all(bf16[8,16,256]{2,1,0:T(8,128)(2,1)S(1)} %bitcast.73), channel_id=1, replica_groups=mesh['vocab'=64,'width'=8] {'width'}, dimensions={0} | all-to-all | bytes 131072 | tf_op jit(solution)/shard_map/all_to_all | solution.py:49
  39.6 0.6 copy.21
  40.3 0.0 all-gather.9.cloned.1.call-start
  40.3 0.7 all-gather.9.cloned.1.call-update
  41.1 1.3 dynamic-slice
  43.0 0.9 dynamic-update-slice
  43.9 22.5 %all-reduce = s32[1024]{0:T(1024)S(1)} all-reduce(s32[1024]{0:T(1024)S(1)} %dynamic-update-slice), channel_id=1, replica_groups=mesh['vocab'=64,'width'=8] {'vocab'}, use_global_device_ids=true, to_apply=%add | all-reduce | flops 1024 | bytes 8192
  66.4 0.7 copy.16
  67.2 0.1 reduce-window.8
  67.3 0.1 reduce
  67.4 0.7 sub.31
  68.0 58.4 %all-gather.7.cloned.1.call-done = bf16[1024,2048]{1,0:T(8,128)(2,1)} async-done(((bf16[16,2048]{1,0:T(8,128)(2,1)}), bf16[1024,2048]{1,0:T(8,128)(2,1)}) %all-gather.7.cloned.1.call-update) | async-done | bytes 4194320 | tf_op jit(solution)/shard_map/all_gather | solution.py:51
  126.4 83.2 %all-gather.9.cloned.1.call-done = bf16[1600,2048]{1,0:T(8,128)(2,1)} async-done(((bf16[1600,256]{1,0:T(8,128)(2,1)}), bf16[1600,2048]{1,0:T(8,128)(2,1)}) %all-gather.9.cloned.1.call-update) | async-done | bytes 6553616 | tf_op jit(solution)/shard_map/all_gather | solution.py:59
  209.6 16.2 %while.32 = (s32[]{:T(128)}, f32[2,512]{1,0:T(2,128)S(1)}, f32[2,512]{1,0:T(2,128)S(1)}, f32[2,512]{1,0:T(2,128)S(1)}, f32[2,512]{1,0:T(2,128)S(1)}, /*index=5*/...) while((s32[]{:T(128)}, f32[2,512]{1,0:T(2,128)S(1)}, ...), condition=%wide.region_7.8_spmd, body=%wide.region_2.7_spmd.sunk | while | flops 3361996288 | bytes 15250565 | solution.py:65
  209.6 6.4 %fusion.14 = (f32[512]{0:T(512)S(1)}, f32[512,1600]{0,1:T(8,128)S(1)}) fusion(bf16[1600,2048]{1,0:T(8,128)(2,1)} %get-tuple-element.320, bf16[2,512,2048]{2,1,0:T(8,128)(2,1)} %get-tuple-element.319, s32[]{:T(128)} %get-tuple-element.303), kind=kOutput, calls=%fused_computation.31.clone.1 | convolution fusion | flops 3356261888 | bytes 11930112 | tf_op jit(solution)/shard_map/while/body/eval_jaxpr/dot_general | solution.py:62
  216.1 1.4 fusion.15
  217.7 6.4 %fusion.14 = (f32[512]{0:T(512)S(1)}, f32[512,1600]{0,1:T(8,128)S(1)}) fusion(bf16[1600,2048]{1,0:T(8,128)(2,1)} %get-tuple-element.320, bf16[2,512,2048]{2,1,0:T(8,128)(2,1)} %get-tuple-element.319, s32[]{:T(128)} %get-tuple-element.303), kind=kOutput, calls=%fused_computation.31.clone.1 | convolution fusion | flops 3356261888 | bytes 11930112 | tf_op jit(solution)/shard_map/while/body/eval_jaxpr/dot_general | solution.py:62
  224.2 1.4 fusion.15
  225.8 42.7 %all-gather = f32[64,1,1024]{2,1,0:T(1,128)S(1)} all-gather(f32[1,1,1024]{2,1,0:T(1,128)S(1)} %reshape.60), channel_id=1, replica_groups=mesh['vocab'=64,'width'=8] {'vocab'}, dimensions={0}, use_global_device_ids=true | all-gather | bytes 266240 | tf_op jit(solution)/shard_map/all_gather | solution.py:11
  268.6 37.2 %all-gather.1 = f32[64,1,1024]{2,1,0:T(1,128)S(1)} all-gather(f32[1,1,1024]{2,1,0:T(1,128)S(1)} %reshape.62), channel_id=1, replica_groups=mesh['vocab'=64,'width'=8] {'vocab'}, dimensions={0}, use_global_device_ids=true | all-gather | bytes 266240 | tf_op jit(solution)/shard_map/all_gather | solution.py:11
  305.8 36.9 %all-gather.2 = f32[64,1,1024]{2,1,0:T(1,128)S(1)} all-gather(f32[1,1,1024]{2,1,0:T(1,128)S(1)} %reshape.64), channel_id=1, replica_groups=mesh['vocab'=64,'width'=8] {'vocab'}, dimensions={0}, use_global_device_ids=true | all-gather | bytes 266240 | tf_op jit(solution)/shard_map/all_gather | solution.py:11
  342.7 37.1 %all-gather.3 = f32[64,1,1024]{2,1,0:T(1,128)S(1)} all-gather(f32[1,1,1024]{2,1,0:T(1,128)S(1)} %reshape.66), channel_id=1, replica_groups=mesh['vocab'=64,'width'=8] {'vocab'}, dimensions={0}, use_global_device_ids=true | all-gather | bytes 266240 | tf_op jit(solution)/shard_map/all_gather | solution.py:11
  380.2 7.6 %while.33 = (s32[]{:T(128)}, f32[1024]{0:T(1024)S(1)}, f32[1024]{0:T(1024)S(1)}, f32[1024]{0:T(1024)S(1)}, f32[1024]{0:T(1024)S(1)}, /*index=5*/f32[63,1024]{1,0...) while((s32[]{:T(128)}, f32[1024]{0:T(1024)S(1)}, ...), condition=%wide.region_9.10_spmd, body=%wide.region_8.9_spmd.sunk | while | flops 16386 | bytes 110701 | solution.py:14
  387.7 0.6 subtract_multiply_fusion
  388.3 0.1 select_reduce_fusion.1
  388.4 95.3 %psum.15 = f32[64]{0:T(128)S(1)} all-reduce(f32[64]{0:T(128)S(1)} %select_reduce_fusion.1), channel_id=1, replica_groups=mesh['vocab'=64,'width'=8] {'vocab','width'}, use_global_device_ids=true, to_apply=%region_12.13 | all-reduce | flops 64 | bytes 512 | tf_op jit(solution)/shard_map/psum | solution.py:93
  483.7 0.5 convert_divide_fusion
  (421 shorter events, 4.6 us)
Async XLA Ops:
  7.2 119.3 %all-gather.7.cloned.1.call-start = ((), (), s32[]{:S(2)}) async-start(), calls=%async_computation.1 | async-start | bytes 4259840 | tf_op jit(solution)/shard_map/all_gather | solution.py:51
  40.3 169.3 %all-gather.9.cloned.1.call-start = ((), (), s32[]{:S(2)}) async-start(), calls=%async_computation.2 | async-start | bytes 7372800 | tf_op jit(solution)/shard_map/all_gather | solution.py:59
  225.8 162.0 %copy-start.2 = (s32[16]{0:T(128)S(1)}, s32[16]{0:T(128)}, u32[]{:S(2)}) copy-start(s32[16]{0:T(128)} %param.14) | copy-start | bytes 196
  225.8 257.9 %copy-start.1 = (s32[64]{0:T(128)S(1)}, s32[64]{0:T(128)}, u32[]{:S(2)}) copy-start(s32[64]{0:T(128)} %param.15) | copy-start | bytes 772
  388.3 95.9 %copy-start = (f32[16]{0:T(128)}, f32[16]{0:T(128)S(1)}, u32[]{:S(2)}) copy-start(f32[16]{0:T(128)S(1)} %get-tuple-element.158) | copy-start | bytes 196
Sparse Core Ops, SparseCore 0:
  40.4 85.9 all-gather.6
  128.4 81.1 all-gather.8
where the time goes:
time: 491 us
  blocking collectives  302 us (62%)
  waiting for transfers between devices  142 us (29%)
  between operations  14.9 us (3%)
  matrix products  12.9 us (3%)
  other arithmetic  9.19 us (2%)
  local copies, waits for them, and re-layouts  6.36 us (1%)
    all_gather x4, blocking collectives, merged_2(): pieces = jax.tree.map(lambda part: lax.all_gather(part, axis), value)  154 us
    psum x1, blocking collectives, per_device(): lax.psum(partial_value, ('vocab', 'width')) / lengths.astype(jnp.float32)  95.3 us
    all_gather x1, waiting for transfers between devices, per_device(): head_full = lax.all_gather(head_weight, 'width', axis=1, tiled=True)  83.2 us
    all_gather x1, waiting for transfers between devices, per_device(): lax.all_gather(full_rows, 'vocab', axis=0, tiled=True)  58.4 us
    unnamed x1, blocking collectives  22.5 us
    psum x1, blocking collectives, per_device(): energy = lax.psum(jnp.sum(values * values, axis=1), 'width')  20.3 us
    dot_general x2, matrix products, per_block(): lax.dot_general(inputs[0], head_full, contract, preferred_element_type=jn...  12.9 us
  transfers between devices with their start and end apart: 2, of which 2 were waited for; matrix products, arithmetic and copies ran while one was open for 1% of the time, Pallas kernels for 0%

commit v1 on v0

--- a/solution.py
+++ b/solution.py
@@ -90,7 +90,7 @@
         (token_index[:, None] >= seq_starts[None, :]) & (token_index[:, None] < seq_ends[None, :])
     ).astype(jnp.float32)
     partial_value = jnp.sum(member * token_logprob[:, None], axis=0)
-    seq_score = lax.psum(partial_value, ("vocab", "width")) / lengths.astype(jnp.float32)
+    seq_score = lax.psum(lax.psum(partial_value, "vocab"), "width") / lengths.astype(jnp.float32)
     return (entropy, token_logprob, seq_score)
 
 

time: 491 us -> 536 us (1.092)
  blocking collectives: 302 us -> 342 us
    psum x1 -> x2, blocking collectives: 95.3 us -> 136 us  [the longest x1 123 us: per_device(): lax.psum(partial_value, 'vocab')]
where the time goes in v1:
time: 536 us; the launch traced here: 532 us
  blocking collectives  342 us (64%)
  waiting for transfers between devices  142 us (26%)
  between operations  14.9 us (3%)
  matrix products  12.9 us (2%)
  other arithmetic  9.19 us (2%)
  local copies, waits for them, and re-layouts  6.36 us (1%)
    all_gather x4, blocking collectives, merged_2(): pieces = jax.tree.map(lambda part: lax.all_gather(part, axis), value)  154 us
    psum x1, blocking collectives, per_device(): lax.psum(partial_value, 'vocab')  123 us
    all_gather x1, waiting for transfers between devices, per_device(): head_full = lax.all_gather(head_weight, 'width', axis=1, tiled=True)  83.2 us
    all_gather x1, waiting for transfers between devices, per_device(): lax.all_gather(full_rows, 'vocab', axis=0, tiled=True)  58.4 us
    unnamed x1, blocking collectives  22.5 us
    psum x1, blocking collectives, per_device(): energy = lax.psum(jnp.sum(values * values, axis=1), 'width')  20.3 us
    dot_general x2, matrix products, per_block(): lax.dot_general(inputs[0], head_full, contract, preferred_element_type=jn...  12.9 us
    psum x1, blocking collectives, per_device(): lax.psum(lax.psum(partial_value, 'vocab'), 'width')  12.3 us
  transfers between devices with their start and end apart: 2, of which 2 were waited for; matrix products, arithmetic and copies ran while one was open for 1% of the time, Pallas kernels for 0%

profile of v1, /device:TPU:1, one launch (start us, length us, event | category | flops | bytes accessed | tf_op | source)
XLA Modules:
  0.0 531.5 jit_solution(14616874720523221621)
XLA Ops:
  7.2 0.9 fusion.5
  8.2 20.3 %psum.21 = f32[128]{0:T(128)S(1)} all-reduce(f32[128]{0:T(128)S(1)} %fusion.5), channel_id=1, replica_groups=mesh['vocab'=64,'width'=8] {'width'}, use_global_device_ids=true, to_apply=%region_1.0 | all-reduce | flops 128 | bytes 1024 | tf_op jit(solution)/shard_map/psum | solution.py:44
  28.4 0.7 convert_element_type.18
  29.1 0.9 fusion.7
  30.0 9.6 %all_to_all.19 = bf16[8,16,256]{2,1,0:T(8,128)(2,1)S(1)} all-to-all(bf16[8,16,256]{2,1,0:T(8,128)(2,1)S(1)} %bitcast.73), channel_id=1, replica_groups=mesh['vocab'=64,'width'=8] {'width'}, dimensions={0} | all-to-all | bytes 131072 | tf_op jit(solution)/shard_map/all_to_all | solution.py:49
  39.6 0.6 copy.21
  40.3 0.0 all-gather.9.cloned.1.call-start
  40.3 0.7 all-gather.9.cloned.1.call-update
  41.1 1.3 dynamic-slice
  43.0 0.9 dynamic-update-slice
  43.9 22.5 %all-reduce = s32[1024]{0:T(1024)S(1)} all-reduce(s32[1024]{0:T(1024)S(1)} %dynamic-update-slice), channel_id=1, replica_groups=mesh['vocab'=64,'width'=8] {'vocab'}, use_global_device_ids=true, to_apply=%add | all-reduce | flops 1024 | bytes 8192
  66.4 0.7 copy.16
  67.2 0.1 reduce-window.8
  67.3 0.1 reduce
  67.4 0.7 sub.31
  68.0 58.4 %all-gather.7.cloned.1.call-done = bf16[1024,2048]{1,0:T(8,128)(2,1)} async-done(((bf16[16,2048]{1,0:T(8,128)(2,1)}), bf16[1024,2048]{1,0:T(8,128)(2,1)}) %all-gather.7.cloned.1.call-update) | async-done | bytes 4194320 | tf_op jit(solution)/shard_map/all_gather | solution.py:51
  126.4 83.2 %all-gather.9.cloned.1.call-done = bf16[1600,2048]{1,0:T(8,128)(2,1)} async-done(((bf16[1600,256]{1,0:T(8,128)(2,1)}), bf16[1600,2048]{1,0:T(8,128)(2,1)}) %all-gather.9.cloned.1.call-update) | async-done | bytes 6553616 | tf_op jit(solution)/shard_map/all_gather | solution.py:59
  209.6 16.2 %while.32 = (s32[]{:T(128)}, f32[2,512]{1,0:T(2,128)S(1)}, f32[2,512]{1,0:T(2,128)S(1)}, f32[2,512]{1,0:T(2,128)S(1)}, f32[2,512]{1,0:T(2,128)S(1)}, /*index=5*/...) while((s32[]{:T(128)}, f32[2,512]{1,0:T(2,128)S(1)}, ...), condition=%wide.region_7.8_spmd, body=%wide.region_2.7_spmd.sunk | while | flops 3361996288 | bytes 15250565 | solution.py:65
  209.6 6.4 %fusion.14 = (f32[512]{0:T(512)S(1)}, f32[512,1600]{0,1:T(8,128)S(1)}) fusion(bf16[1600,2048]{1,0:T(8,128)(2,1)} %get-tuple-element.320, bf16[2,512,2048]{2,1,0:T(8,128)(2,1)} %get-tuple-element.319, s32[]{:T(128)} %get-tuple-element.303), kind=kOutput, calls=%fused_computation.31.clone.1 | convolution fusion | flops 3356261888 | bytes 11930112 | tf_op jit(solution)/shard_map/while/body/eval_jaxpr/dot_general | solution.py:62
  216.1 1.4 fusion.15
  217.7 6.4 %fusion.14 = (f32[512]{0:T(512)S(1)}, f32[512,1600]{0,1:T(8,128)S(1)}) fusion(bf16[1600,2048]{1,0:T(8,128)(2,1)} %get-tuple-element.320, bf16[2,512,2048]{2,1,0:T(8,128)(2,1)} %get-tuple-element.319, s32[]{:T(128)} %get-tuple-element.303), kind=kOutput, calls=%fused_computation.31.clone.1 | convolution fusion | flops 3356261888 | bytes 11930112 | tf_op jit(solution)/shard_map/while/body/eval_jaxpr/dot_general | solution.py:62
  224.2 1.4 fusion.15
  225.8 42.7 %all-gather = f32[64,1,1024]{2,1,0:T(1,128)S(1)} all-gather(f32[1,1,1024]{2,1,0:T(1,128)S(1)} %reshape.60), channel_id=1, replica_groups=mesh['vocab'=64,'width'=8] {'vocab'}, dimensions={0}, use_global_device_ids=true | all-gather | bytes 266240 | tf_op jit(solution)/shard_map/all_gather | solution.py:11
  268.6 37.2 %all-gather.1 = f32[64,1,1024]{2,1,0:T(1,128)S(1)} all-gather(f32[1,1,1024]{2,1,0:T(1,128)S(1)} %reshape.62), channel_id=1, replica_groups=mesh['vocab'=64,'width'=8] {'vocab'}, dimensions={0}, use_global_device_ids=true | all-gather | bytes 266240 | tf_op jit(solution)/shard_map/all_gather | solution.py:11
  305.8 36.9 %all-gather.2 = f32[64,1,1024]{2,1,0:T(1,128)S(1)} all-gather(f32[1,1,1024]{2,1,0:T(1,128)S(1)} %reshape.64), channel_id=1, replica_groups=mesh['vocab'=64,'width'=8] {'vocab'}, dimensions={0}, use_global_device_ids=true | all-gather | bytes 266240 | tf_op jit(solution)/shard_map/all_gather | solution.py:11
  342.7 37.1 %all-gather.3 = f32[64,1,1024]{2,1,0:T(1,128)S(1)} all-gather(f32[1,1,1024]{2,1,0:T(1,128)S(1)} %reshape.66), channel_id=1, replica_groups=mesh['vocab'=64,'width'=8] {'vocab'}, dimensions={0}, use_global_device_ids=true | all-gather | bytes 266240 | tf_op jit(solution)/shard_map/all_gather | solution.py:11
  380.2 7.6 %while.33 = (s32[]{:T(128)}, f32[1024]{0:T(1024)S(1)}, f32[1024]{0:T(1024)S(1)}, f32[1024]{0:T(1024)S(1)}, f32[1024]{0:T(1024)S(1)}, /*index=5*/f32[63,1024]{1,0...) while((s32[]{:T(128)}, f32[1024]{0:T(1024)S(1)}, ...), condition=%wide.region_9.10_spmd, body=%wide.region_8.9_spmd.sunk | while | flops 16386 | bytes 110701 | solution.py:14
  387.7 0.6 subtract_multiply_fusion
  388.3 0.1 select_reduce_fusion.1
  388.4 123.4 %psum.22 = f32[64]{0:T(128)S(1)} all-reduce(f32[64]{0:T(128)S(1)} %select_reduce_fusion.1), channel_id=1, replica_groups=mesh['vocab'=64,'width'=8] {'vocab'}, use_global_device_ids=true, to_apply=%region_12.13 | all-reduce | flops 64 | bytes 512 | tf_op jit(solution)/shard_map/psum | solution.py:93
  511.8 12.3 %psum.23 = f32[64]{0:T(128)S(1)} all-reduce(f32[64]{0:T(128)S(1)} %psum.22), channel_id=1, replica_groups=mesh['vocab'=64,'width'=8] {'width'}, use_global_device_ids=true, to_apply=%region_13.14 | all-reduce | flops 64 | bytes 512 | tf_op jit(solution)/shard_map/psum | solution.py:93
  524.1 0.5 convert_divide_fusion
  (422 shorter events, 4.7 us)
Async XLA Ops:
  7.2 119.3 %all-gather.7.cloned.1.call-start = ((), (), s32[]{:S(2)}) async-start(), calls=%async_computation.1 | async-start | bytes 4259840 | tf_op jit(solution)/shard_map/all_gather | solution.py:51
  40.3 169.3 %all-gather.9.cloned.1.call-start = ((), (), s32[]{:S(2)}) async-start(), calls=%async_computation.2 | async-start | bytes 7372800 | tf_op jit(solution)/shard_map/all_gather | solution.py:59
  225.8 162.0 %copy-start.2 = (s32[16]{0:T(128)S(1)}, s32[16]{0:T(128)}, u32[]{:S(2)}) copy-start(s32[16]{0:T(128)} %param.14) | copy-start | bytes 196
  225.8 298.4 %copy-start.1 = (s32[64]{0:T(128)S(1)}, s32[64]{0:T(128)}, u32[]{:S(2)}) copy-start(s32[64]{0:T(128)} %param.15) | copy-start | bytes 772
  388.3 136.3 %copy-start = (f32[16]{0:T(128)}, f32[16]{0:T(128)S(1)}, u32[]{:S(2)}) copy-start(f32[16]{0:T(128)S(1)} %get-tuple-element.158) | copy-start | bytes 196
Sparse Core Ops, SparseCore 0:
  40.4 85.9 all-gather.6
  128.4 81.1 all-gather.8
